TPU v7x, 32 devices: a whole 2x2x4 slice. The times are simulated.
32 devices in a mesh: freq: 4 (over y, x), param: 8 (over z, core).
Axes of the slice: x: 2, y: 2, z: 4, core: 2. Of those that a mesh axis runs over, the one named last changes fastest.
Arguments:
- chain_state: float32 [32, 2048, 512], P('freq', 'param'), may hold values from -6 to 6
- second_moment: float32 [32, 2048, 512], P('freq', 'param'), may hold values from 0.25 to 2
- noise: float32 [2, 32, 2048, 512], P(None, 'freq', 'param'), may hold values from -6 to 6
- green: bfloat16 [2, 64, 2048, 512], P(None, 'freq', 'param'), may hold values from -0.125 to 0.125
- observed: float32 [64, 1024], P('freq'), may hold values from -6 to 6
- inv_noise: float32 [64, 512], P('freq'), may hold values from 0.3 to 3
- temper: float32 [32], P('freq'), may hold values from 0.2 to 1
Outputs:
- new_state: float32 [32, 2048, 512], P('freq', 'param')
- new_moment: float32 [32, 2048, 512], P('freq', 'param')
All inputs are finite; a program needn't handle non-finite values.
Results may differ from a plain program's by a relative error of at most 0.005.
Values may be sent and summed in bfloat16 or wider, within the bound.
A program may use at most 128 MiB of HBM per device.

v0:
```python
import math

import jax
import jax.numpy as jnp
from jax import lax
from jax.sharding import PartitionSpec as P

decay_rate = 0.9
step_length = 0.5


def spectral_table(time_len, freq_total):
    time_index = jnp.arange(time_len, dtype=jnp.int32)[:, None]
    wave_number = jnp.arange(freq_total, dtype=jnp.int32)[None, :] + 1
    phase_angle = (time_index * wave_number % time_len).astype(jnp.float32) * (
        2.0 * math.pi / time_len
    )
    columns_table = jnp.stack([jnp.cos(phase_angle), -jnp.sin(phase_angle)], axis=-1).reshape(
        time_len, 2 * freq_total
    )
    return (columns_table / math.sqrt(time_len)).astype(jnp.bfloat16)


def on_device(chain_state, second_moment, noise, green, observed, inv_noise, temper):
    chains_loc, slab_rows, time_len = chain_state.shape
    freq_loc = green.shape[1]
    freq_count = lax.axis_size("freq")
    freq_total = freq_loc * freq_count
    chains = chains_loc * freq_count
    forward_table = spectral_table(time_len, freq_total)
    inverse_table = forward_table.T
    green_re = green[0]
    green_im = green[1]
    upper_rows = jnp.concatenate([green_re, green_im], axis=2)
    lower_rows = jnp.concatenate([-green_im, green_re], axis=2)
    kernel = jnp.concatenate([upper_rows, lower_rows], axis=1)
    weights = jnp.concatenate([inv_noise, inv_noise], axis=1)
    temper_cols = temper[:, None, None]
    current = chain_state
    moment = second_moment
    for step_num in range(noise.shape[0]):
        low_state = current.astype(jnp.bfloat16)
        local_spec = jnp.dot(
            low_state.reshape(chains_loc * slab_rows, time_len),
            forward_table,
            preferred_element_type=jnp.float32,
        )
        local_spec = local_spec.astype(jnp.bfloat16).reshape(chains_loc, slab_rows, 2 * freq_total)
        spectrum = lax.all_to_all(local_spec, "freq", split_axis=2, concat_axis=0, tiled=True)
        mixed_spec = (
            spectrum.reshape(chains, slab_rows, freq_loc, 2)
            .transpose(2, 0, 3, 1)
            .reshape(freq_loc, chains, 2 * slab_rows)
        )
        partial_data = jnp.einsum(
            "fcq,fqs->fcs", mixed_spec, kernel, preferred_element_type=jnp.float32
        )
        predicted = lax.psum(partial_data.astype(jnp.bfloat16), "param").astype(jnp.float32)
        weighted = (weights[:, None, :] * (predicted - observed[:, None, :])).astype(jnp.bfloat16)
        adjoint = jnp.einsum(
            "fcs,fqs->fcq", weighted, kernel, preferred_element_type=jnp.float32
        ).astype(jnp.bfloat16)
        adjoint = (
            adjoint.reshape(freq_loc, chains, 2, slab_rows)
            .transpose(1, 3, 0, 2)
            .reshape(chains, slab_rows, 2 * freq_loc)
        )
        own_adjoint = lax.all_to_all(adjoint, "freq", split_axis=0, concat_axis=2, tiled=True)
        gradient = jnp.dot(
            own_adjoint.reshape(chains_loc * slab_rows, 2 * freq_total),
            inverse_table,
            preferred_element_type=jnp.float32,
        )
        gradient = gradient.reshape(chains_loc, slab_rows, time_len)
        drift_term = temper_cols * gradient + current
        moment = decay_rate * moment + (1.0 - decay_rate) * drift_term * drift_term
        precondition = lax.rsqrt(moment)
        current = (
            current
            - step_length * precondition * drift_term
            + math.sqrt(2.0 * step_length) * jnp.sqrt(precondition) * noise[step_num]
        )
    return (current, moment)


def solution(mesh):
    return jax.shard_map(
        on_device,
        mesh=mesh,
        in_specs=(
            P("freq", "param", None),
            P("freq", "param", None),
            P(None, "freq", "param", None),
            P(None, "freq", "param", None),
            P("freq", None),
            P("freq", None),
            P("freq"),
        ),
        out_specs=(P("freq", "param", None), P("freq", "param", None)),
        check_vma=False,
    )
```

profile of v0, /device:TPU:0, one launch (start us, length us, event | category | flops | bytes accessed | tf_op | source)
XLA Modules:
  0.0 238.1 jit_solution(13732761810308003860)
XLA Ops:
  7.2 0.6 fusion.19
  7.8 0.1 copy.56
  7.9 0.1 convert_element_type.81
  8.0 2.5 %convert_element_type.82 = bf16[8,256,512]{2,1,0:T(8,128)(2,1)S(1)} convert(f32[8,256,512]{2,1,0:T(8,128)} %param.7) | non-fusion elementwise | flops 1048576 | bytes 6291456 | tf_op jit(solution)/shard_map/convert_element_type | solution.py:42
  10.5 0.8 convolution_convert_fusion.1
  11.3 0.9 copy.86
  12.2 5.2 %all-to-all-start = ((bf16[8,256,128]{1,0,2:T(8,128)(2,1)}), bf16[8,256,128]{1,0,2:T(8,128)(2,1)S(1)}, u32[]{:S(2)}, u32[]{:S(2)}) async-start(bf16[8,256,128]{1,0,2:T(8,128)(2,1)} %bitcast.48), calls=%async_computation | async-start | bytes 1048576 | tf_op jit(solution)/shard_map/all_to_all | solution.py:49
  17.4 0.0 all-reduce.3.cloned.1.call-start
  17.4 5.9 %slice_bitcast_fusion = (bf16[16,256,512]{2,1,0:T(8,128)(2,1)}, bf16[16,256,512]{2,1,0:T(8,128)(2,1)}) fusion(bf16[2,16,256,512]{3,2,1,0:T(8,128)(2,1)} %param.10), kind=kLoop, calls=%fused_computation.11 | loop fusion | bytes 16777216 | tf_op jit(solution)/shard_map/squeeze | solution.py:33
  23.3 4.4 %fusion.20 = bf16[16,256,512]{2,1,0:T(8,128)(2,1)} fusion(bf16[2,16,256,512]{3,2,1,0:T(8,128)(2,1)} %param.10), kind=kLoop, calls=%fused_computation.46 | loop fusion | flops 2097152 | bytes 8388608 | tf_op jit(solution)/shard_map/neg | solution.py:35
  27.7 0.0 all-to-all-done
  27.8 0.0 copy-start.2
  27.8 0.0 copy-start.4
  27.8 8.4 %convolution_convert_fusion.3 = bf16[16,32,1024]{2,1,0:T(8,128)(2,1)} fusion(bf16[16,32,512]{2,1,0:T(8,128)(2,1)S(1)} %bitcast.98, bf16[16,256,512]{2,1,0:T(8,128)(2,1)} %get-tuple-element.7, bf16[16,256,512]{2,1,0:T(8,128)(2,1)} %fusion.20, bf16[16,256,512]{2,1,0:T(8,128)(2,1)} %get-tuple-element.6), kind=kOutput, calls=%fused_computation.18 | convolution fusion | flops 604504064 | bytes 14155776 | tf_op jit(solution)/shard_map/fcq,fqs->fcs/dot_general | solution.py:55
  36.3 0.0 all-reduce.3.cloned.1.call-update
  36.3 0.0 all-reduce.5.cloned.1.call-start
  36.3 0.0 copy-done.2
  36.4 61.1 %all-reduce.3.cloned.1.call-done = bf16[16,32,1024]{2,1,0:T(8,128)(2,1)} async-done(((bf16[16,32,1024]{2,1,0:T(8,128)(2,1)}), bf16[16,32,1024]{2,1,0:T(8,128)(2,1)}) %all-reduce.3.cloned.1.call-update) | async-done | bytes 1048592 | tf_op jit(solution)/shard_map/psum | solution.py:58
  97.5 0.0 copy-done.4
  97.5 8.7 %convolution_convert_fusion.5 = bf16[16,32,512]{2,1,0:T(8,128)(2,1)S(1)} fusion(bf16[16,32,1024]{2,1,0:T(8,128)(2,1)} %all-reduce.3.cloned.1.call-done, f32[16,1024]{1,0:T(8,128)S(1)} %copy-done.4, f32[16,1024]{1,0:T(8,128)S(1)} %pad_maximum_fusion, bf16[16,256,512]{2,1,0:T(8,128)(2,1)} %get-tuple-element.7, bf16[16,256,512]{2,1,0:T(8,128)(2,1)} %fusion.20, ...), kind=kOutput, calls=%fused_computation.20 | convolution fusion | flops 606339072 | bytes 14286848 | tf_op jit(solution)/shard_map/fcs,fqs->fcq/dot_general | solution.py:60
  106.2 0.0 copy-start
  106.2 0.0 copy-start.3
  106.3 0.1 copy.92
  106.3 0.3 copy.61
  106.6 10.8 %all_to_all.60 = bf16[32,256,32]{1,2,0:T(8,128)(2,1)S(1)} all-to-all(bf16[32,256,32]{1,2,0:T(8,128)(2,1)S(1)} %copy.61), channel_id=1, replica_groups=mesh['freq'=4,'param'=8] {'freq'}, dimensions={0} | all-to-all | bytes 1048576 | tf_op jit(solution)/shard_map/all_to_all | solution.py:68
  117.4 0.0 copy-done
  117.5 0.0 copy-done.3
  117.5 7.4 %fusion.22 = (bf16[8,256,512]{2,1,0:T(8,128)(2,1)S(1)}, f32[8,256,512]{2,1,0:T(8,128)}, f32[8,256,512]{2,1,0:T(8,128)}) fusion(f32[2,8,256,512]{3,2,1,0:T(8,128)} %param.9, f32[8,256,512]{2,1,0:T(8,128)S(1)} %copy-done, f32[8]{0:T(128)S(1)} %copy-done.3, f32[8,256,512]{2,1,0:T(8,128)} %param.8, bf16[8,256,128]{1,2,0:T(8,128)(2,1)S(1)} %bitcast.88, ...), kind=kOutput, calls=%fused_computation.47 | convolution fusion | flops 281018368 | bytes 23724064 | tf_op jit(solution)/shard_map/dot_general | solution.py:69
  124.8 0.7 convolution_convert_fusion
  125.5 0.4 copy.65
  125.9 9.5 %all_to_all.61 = bf16[8,256,128]{1,0,2:T(8,128)(2,1)S(1)} all-to-all(bf16[8,256,128]{1,0,2:T(8,128)(2,1)S(1)} %copy.65), channel_id=1, replica_groups=mesh['freq'=4,'param'=8] {'freq'}, dimensions={2} | all-to-all | bytes 1048576 | tf_op jit(solution)/shard_map/all_to_all | solution.py:49
  135.5 8.4 %convolution_convert_fusion.2 = bf16[16,32,1024]{2,1,0:T(8,128)(2,1)} fusion(bf16[16,32,512]{2,1,0:T(8,128)(2,1)S(1)} %bitcast.100, bf16[16,256,512]{2,1,0:T(8,128)(2,1)} %get-tuple-element.7, bf16[16,256,512]{2,1,0:T(8,128)(2,1)} %fusion.20, bf16[16,256,512]{2,1,0:T(8,128)(2,1)} %get-tuple-element.6), kind=kOutput, calls=%fused_computation.17 | convolution fusion | flops 604504064 | bytes 14155776 | tf_op jit(solution)/shard_map/fcq,fqs->fcs/dot_general | solution.py:55
  143.9 0.0 all-reduce.5.cloned.1.call-update
  144.0 57.5 %all-reduce.5.cloned.1.call-done = bf16[16,32,1024]{2,1,0:T(8,128)(2,1)} async-done(((bf16[16,32,1024]{2,1,0:T(8,128)(2,1)}), bf16[16,32,1024]{2,1,0:T(8,128)(2,1)}) %all-reduce.5.cloned.1.call-update) | async-done | bytes 1048592 | tf_op jit(solution)/shard_map/psum | solution.py:58
  201.5 8.8 %convolution_convert_fusion.4 = bf16[16,32,512]{2,1,0:T(8,128)(2,1)S(1)} fusion(bf16[16,32,1024]{2,1,0:T(8,128)(2,1)} %all-reduce.5.cloned.1.call-done, f32[16,1024]{1,0:T(8,128)S(1)} %copy-done.4, f32[16,1024]{1,0:T(8,128)S(1)} %pad_maximum_fusion, bf16[16,256,512]{2,1,0:T(8,128)(2,1)} %get-tuple-element.7, bf16[16,256,512]{2,1,0:T(8,128)(2,1)} %fusion.20, ...), kind=kOutput, calls=%fused_computation.19 | convolution fusion | flops 606339072 | bytes 14286848 | tf_op jit(solution)/shard_map/fcs,fqs->fcq/dot_general | solution.py:60
  210.3 0.0 copy-start.1
  210.3 0.1 copy.91
  210.4 0.3 copy.70
  210.7 10.8 %all_to_all.62 = bf16[32,256,32]{1,2,0:T(8,128)(2,1)S(1)} all-to-all(bf16[32,256,32]{1,2,0:T(8,128)(2,1)S(1)} %copy.70), channel_id=1, replica_groups=mesh['freq'=4,'param'=8] {'freq'}, dimensions={0} | all-to-all | bytes 1048576 | tf_op jit(solution)/shard_map/all_to_all | solution.py:68
  221.5 0.0 copy-done.1
  221.5 9.7 %fusion.2 = (f32[8,256,512]{2,1,0:T(8,128)}, f32[8,256,512]{2,1,0:T(8,128)}) fusion(f32[2,8,256,512]{3,2,1,0:T(8,128)} %param.9, f32[8,256,512]{2,1,0:T(8,128)} %get-tuple-element.5, f32[8]{0:T(128)S(1)} %copy-done.3, f32[8,256,512]{2,1,0:T(8,128)S(1)} %copy-done.1, f32[8,256,512]{2,1,0:T(8,128)} %get-tuple-element.10, f32[8,256,512]{2,1,0:T(8,128)} %param.8, ...), kind=kOutput, calls=%fused_computation.6 | convolution fusion | flops 286261248 | bytes 30015520 | tf_op jit(solution)/shard_map/dot_general | solution.py:69
  (7 shorter events, 0.2 us)
Async XLA Ops:
  12.2 15.5 %all-to-all-start = ((bf16[8,256,128]{1,0,2:T(8,128)(2,1)}), bf16[8,256,128]{1,0,2:T(8,128)(2,1)S(1)}, u32[]{:S(2)}, u32[]{:S(2)}) async-start(bf16[8,256,128]{1,0,2:T(8,128)(2,1)} %bitcast.48), calls=%async_computation | async-start | bytes 1048576 | tf_op jit(solution)/shard_map/all_to_all | solution.py:49
  17.4 80.1 %all-reduce.3.cloned.1.call-start = ((), (), s32[]{:S(2)}) async-start(), calls=%async_computation.4 | async-start | bytes 2097152 | tf_op jit(solution)/shard_map/psum | solution.py:58
  27.8 8.5 %copy-start.2 = (f32[16,512]{1,0:T(8,128)S(1)}, f32[16,512]{1,0:T(8,128)}, u32[]{:S(2)}) copy-start(f32[16,512]{1,0:T(8,128)} %param.12) | copy-start | bytes 98308
  27.8 69.7 %copy-start.4 = (f32[16,1024]{1,0:T(8,128)S(1)}, f32[16,1024]{1,0:T(8,128)}, u32[]{:S(2)}) copy-start(f32[16,1024]{1,0:T(8,128)} %param.11) | copy-start | bytes 196612
  36.3 165.2 %all-reduce.5.cloned.1.call-start = ((), (), s32[]{:S(2)}) async-start(), calls=%async_computation.5 | async-start | bytes 2097152 | tf_op jit(solution)/shard_map/psum | solution.py:58
  106.2 11.2 %copy-start = (f32[8,256,512]{2,1,0:T(8,128)S(1)}, f32[8,256,512]{2,1,0:T(8,128)}, u32[]{:S(2)}) copy-start(f32[8,256,512]{2,1,0:T(8,128)} %param.7) | copy-start | bytes 12582916
  106.2 11.2 %copy-start.3 = (f32[8]{0:T(128)S(1)}, f32[8]{0:T(128)}, u32[]{:S(2)}) copy-start(f32[8]{0:T(128)} %param.13) | copy-start | bytes 100
  210.3 11.2 %copy-start.1 = (f32[8,256,512]{2,1,0:T(8,128)S(1)}, f32[8,256,512]{2,1,0:T(8,128)}, u32[]{:S(2)}) copy-start(f32[8,256,512]{2,1,0:T(8,128)} %param.7) | copy-start | bytes 12582916
Sparse Core Ops, SparseCore 0:
  36.4 61.0 all-reduce.2
  144.1 57.3 all-reduce.4
where the time goes:
time: 238 us
  waiting for transfers between devices  119 us (50%)
  matrix products  53.1 us (22%)
  blocking collectives  31.1 us (13%)
  between operations  14.2 us (6%)
  local copies, waits for them, and re-layouts  8.32 us (3%)
  other arithmetic  7.49 us (3%)
  starting transfers between devices  5.23 us (2%)
    psum x2, waiting for transfers between devices, on_device(): lax.psum(partial_data.astype(jnp.bfloat16), 'param').astype(jnp.float32)  119 us
    all_to_all x2, blocking collectives, on_device(): lax.all_to_all(adjoint, 'freq', split_axis=0, concat_axis=2, tiled=True)  21.6 us
    dot_general x2, matrix products, on_device(): jnp.einsum('fcs,fqs->fcq', weighted, kernel, preferred_element_type=jnp.f...  17.6 us
    dot_general x2, matrix products, on_device(): jnp.dot(own_adjoint.reshape(chains_loc * slab_rows, 2 * freq_total), inve...  17.1 us
    dot_general x2, matrix products, on_device(): jnp.einsum('fcq,fqs->fcs', mixed_spec, kernel, preferred_element_type=jnp...  16.9 us
    all_to_all x1, blocking collectives, on_device(): lax.all_to_all(local_spec, 'freq', split_axis=2, concat_axis=0, tiled=True)  9.53 us
    squeeze x1, local copies, waits for them, and re-layouts, on_device(): green_im = green[1]  5.93 us
    all_to_all x1, starting transfers between devices, on_device(): lax.all_to_all(local_spec, 'freq', split_axis=2, concat_axis=0, tiled=True)  5.19 us
  transfers between devices with their start and end apart: 3, of which 2 were waited for; matrix products, arithmetic and copies ran while one was open for 4% of the time, Pallas kernels for 0%

commit v1 on v0

--- a/solution.py
+++ b/solution.py
@@ -1,12 +1,18 @@
+import functools
 import math
 
 import jax
 import jax.numpy as jnp
 from jax import lax
+from jax.experimental import pallas as pl
+from jax.experimental.pallas import tpu as pltpu
 from jax.sharding import PartitionSpec as P
 
 decay_rate = 0.9
 step_length = 0.5
+MESH = pl.DeviceIdType.MESH
+LANES = 128
+CHUNK_FREQS = 2
 
 
 def spectral_table(time_len, freq_total):
@@ -21,7 +27,330 @@
     return (columns_table / math.sqrt(time_len)).astype(jnp.bfloat16)
 
 
+def exchange_kernel(
+    freq_count, levels, chunk_freqs,
+    spec_ref, green_hbm, obs_ref, inv_ref, own_ref,
+    green, field, acc, outgoing, incoming, wtd, adj,
+    green_sem, spec_send, spec_recv, red_send, red_recv, gat_send, gat_recv,
+    adj_send, adj_recv, local_sem,
+):
+    freq_me = lax.axis_index("freq")
+    param_me = lax.axis_index("param")
+    freq_loc, rows = spec_ref.shape[1], spec_ref.shape[2]
+    half_rows = rows // 2
+    sensors = green.shape[3]
+    col_blocks = sensors // LANES
+    chunk_blocks = chunk_freqs * col_blocks
+    chunks = freq_loc // chunk_freqs
+    bits = [lax.rem(param_me // 2**k, 2) for k in range(levels)]
+    partners = [param_me + (1 - 2 * bits[k]) * 2**k for k in range(levels)]
+    lens = [chunk_blocks // 2**k for k in range(levels + 1)]
+    offs = [0]
+    for k in range(levels):
+        offs.append(offs[k] + bits[k] * lens[k + 1])
+
+    def freq_peer(d):
+        return lax.rem(freq_me + d, freq_count)
+
+    def freq_source(d):
+        return lax.rem(freq_me + freq_count - d, freq_count)
+
+    barrier = pltpu.get_barrier_semaphore()
+    for d in range(1, freq_count):
+        pl.semaphore_signal(barrier, inc=1, device_id={"freq": freq_peer(d)}, device_id_type=MESH)
+    for k in range(levels):
+        pl.semaphore_signal(barrier, inc=1, device_id={"param": partners[k]}, device_id_type=MESH)
+
+    def green_copy(i):
+        part = pl.ds(i * chunk_freqs, chunk_freqs)
+        return pltpu.make_async_copy(green_hbm.at[:, part], green.at[:, part], green_sem.at[i])
+
+    def own_spec_copy():
+        return pltpu.make_async_copy(spec_ref.at[freq_me], field.at[:, freq_me], local_sem.at[0])
+
+    def spec_copy(i, d):
+        part = pl.ds(i * chunk_freqs, chunk_freqs)
+        return pltpu.make_async_remote_copy(
+            src_ref=spec_ref.at[freq_peer(d), part],
+            dst_ref=field.at[part, freq_me],
+            send_sem=spec_send.at[d - 1, i],
+            recv_sem=spec_recv.at[d - 1, i],
+            device_id={"freq": freq_peer(d)},
+            device_id_type=MESH,
+        )
+
+    def reduce_copy(i, k):
+        part = pl.ds(i * lens[k + 1], lens[k + 1])
+        if k == 0:
+            away = (1 - bits[0]) * lens[1]
+            src = outgoing[0].at[pl.ds(i * chunk_blocks + away, lens[1])]
+        else:
+            src = outgoing[k].at[part]
+        return pltpu.make_async_remote_copy(
+            src_ref=src,
+            dst_ref=incoming[k].at[part],
+            send_sem=red_send.at[k, i],
+            recv_sem=red_recv.at[k, i],
+            device_id={"param": partners[k]},
+            device_id_type=MESH,
+        )
+
+    def gather_copy(i, k):
+        part = pl.ds(i * chunk_blocks + offs[k + 1], lens[k + 1])
+        return pltpu.make_async_remote_copy(
+            src_ref=wtd.at[part],
+            dst_ref=wtd.at[part],
+            send_sem=gat_send.at[k, i],
+            recv_sem=gat_recv.at[k, i],
+            device_id={"param": partners[k]},
+            device_id_type=MESH,
+        )
+
+    def adj_copy(i, d):
+        part = pl.ds(i * chunk_freqs, chunk_freqs)
+        return pltpu.make_async_remote_copy(
+            src_ref=adj.at[part, freq_peer(d)],
+            dst_ref=own_ref.at[freq_me, part],
+            send_sem=adj_send.at[d - 1, i],
+            recv_sem=adj_recv.at[d - 1, i],
+            device_id={"freq": freq_peer(d)},
+            device_id_type=MESH,
+        )
+
+    def own_adj_copy(i):
+        part = pl.ds(i * chunk_freqs, chunk_freqs)
+        return pltpu.make_async_copy(
+            adj.at[part, freq_me], own_ref.at[freq_me, part], local_sem.at[i + 1]
+        )
+
+    own_spec_copy().start()
+
+    @pl.loop(0, chunks)
+    def _(i):
+        green_copy(i).start()
+
+    pl.semaphore_wait(barrier, freq_count - 1 + levels)
+
+    @pl.loop(0, chunks)
+    def _(i):
+        for d in range(1, freq_count):
+            spec_copy(i, d).start()
+
+    own_spec_copy().wait()
+
+    def combine(first, second, sign):
+        pieces = []
+        for j in range(freq_count):
+            for ri in range(2):
+                here = j * rows + ri * half_rows
+                there = j * rows + (1 - ri) * half_rows
+                a = first[here : here + half_rows]
+                b = second[there : there + half_rows]
+                pieces.append(a + b if (ri == 1) == (sign > 0) else a - b)
+        return jnp.concatenate(pieces, axis=0)
+
+    def forward(i):
+        green_copy(i).wait()
+        for d in range(1, freq_count):
+            spec_copy(i, d).wait_recv()
+        for g in range(chunk_freqs):
+            f = i * chunk_freqs + g
+            x = field[f].reshape(freq_count * rows, field.shape[3])
+            first = jnp.dot(x, green[0, f], preferred_element_type=jnp.float32)
+            second = jnp.dot(x, green[1, f], preferred_element_type=jnp.float32)
+            data = combine(first, second, 1)
+            for b in range(col_blocks):
+                block = data[:, b * LANES : (b + 1) * LANES]
+                acc[f * col_blocks + b] = block
+                outgoing[0][f * col_blocks + b] = block.astype(jnp.bfloat16)
+        reduce_copy(i, 0).start()
+
+    def reduce(i, k):
+        reduce_copy(i, k - 1).wait_recv()
+        kept = pl.ds(i * chunk_blocks + offs[k], lens[k])
+        acc[kept] = acc[kept] + incoming[k - 1][pl.ds(i * lens[k], lens[k])].astype(jnp.float32)
+        away = offs[k] + (1 - bits[k]) * lens[k + 1]
+        outgoing[k][pl.ds(i * lens[k + 1], lens[k + 1])] = acc[
+            pl.ds(i * chunk_blocks + away, lens[k + 1])
+        ].astype(jnp.bfloat16)
+        reduce_copy(i, k).start()
+
+    def weigh(i):
+        reduce_copy(i, levels - 1).wait_recv()
+        for n in range(lens[levels]):
+            b = i * chunk_blocks + offs[levels] + n
+            total = acc[b] + incoming[levels - 1][i * lens[levels] + n].astype(jnp.float32)
+            target = obs_ref[b]
+            weight = inv_ref[b]
+            pieces = []
+            for j in range(freq_count):
+                for ri in range(2):
+                    here = j * rows + ri * half_rows
+                    pieces.append(
+                        weight * (total[here : here + half_rows] - target[ri : ri + 1])
+                    )
+            wtd[b] = jnp.concatenate(pieces, axis=0).astype(jnp.bfloat16)
+        gather_copy(i, levels - 1).start()
+
+    def gather(i, k):
+        gather_copy(i, k).wait_recv()
+        gather_copy(i, k - 1).start()
+
+    def backward(i):
+        gather_copy(i, 0).wait_recv()
+        dims = (((1,), (1,)), ((), ()))
+        for g in range(chunk_freqs):
+            f = i * chunk_freqs + g
+            w = jnp.concatenate([wtd[f * col_blocks + b] for b in range(col_blocks)], axis=1)
+            first = lax.dot_general(w, green[0, f], dims, preferred_element_type=jnp.float32)
+            second = lax.dot_general(w, green[1, f], dims, preferred_element_type=jnp.float32)
+            back = combine(first, second, -1).astype(jnp.bfloat16)
+            adj[f] = back.reshape(freq_count, rows, back.shape[1])
+        for d in range(1, freq_count):
+            adj_copy(i, d).start()
+        own_adj_copy(i).start()
+
+    stages = [forward]
+    for k in range(1, levels):
+        stages.append(functools.partial(reduce, k=k))
+    stages.append(weigh)
+    for k in range(levels - 1, 0, -1):
+        stages.append(functools.partial(gather, k=k))
+    stages.append(backward)
+
+    @pl.loop(0, chunks + len(stages) - 1)
+    def _(tick):
+        for lag, stage in enumerate(stages):
+            @pl.when((tick >= lag) & (tick < chunks + lag))
+            def _():
+                stage(tick - lag)
+
+    @pl.loop(0, chunks)
+    def _(i):
+        for d in range(1, freq_count):
+            spec_copy(i, d).wait_send()
+        for k in range(levels):
+            reduce_copy(i, k).wait_send()
+            gather_copy(i, k).wait_send()
+        for d in range(1, freq_count):
+            adj_copy(i, d).wait_send()
+            adj_copy(i, d).wait_recv()
+        own_adj_copy(i).wait()
+
+
+def exchange(spec, green, obs_blocks, inv_blocks, call_id):
+    freq_count, freq_loc, rows, slab = spec.shape
+    levels = int(math.log2(lax.axis_size("param")))
+    sensors = green.shape[3]
+    col_blocks = sensors // LANES
+    chunk_blocks = CHUNK_FREQS * col_blocks
+    chunks = freq_loc // CHUNK_FREQS
+    blocks = freq_loc * col_blocks
+    all_rows = freq_count * rows
+    bf16, f32 = jnp.bfloat16, jnp.float32
+    piece = [blocks // 2 ** (k + 1) for k in range(levels)]
+    dma = pltpu.SemaphoreType.DMA
+    vmem = pl.BlockSpec(memory_space=pltpu.VMEM)
+    flops = 16 * freq_loc * all_rows * slab * sensors
+    return pl.pallas_call(
+        functools.partial(exchange_kernel, freq_count, levels, CHUNK_FREQS),
+        out_shape=jax.ShapeDtypeStruct(spec.shape, bf16),
+        in_specs=[vmem, pl.BlockSpec(memory_space=pl.ANY), vmem, vmem],
+        out_specs=vmem,
+        scratch_shapes=[
+            pltpu.VMEM(green.shape, bf16),
+            pltpu.VMEM((freq_loc, freq_count, rows, slab), bf16),
+            pltpu.VMEM((blocks, all_rows, LANES), f32),
+            [
+                pltpu.VMEM((blocks if k == 0 else piece[k], all_rows, LANES), bf16)
+                for k in range(levels)
+            ],
+            [pltpu.VMEM((piece[k], all_rows, LANES), bf16) for k in range(levels)],
+            pltpu.VMEM((blocks, all_rows, LANES), bf16),
+            pltpu.VMEM((freq_loc, freq_count, rows, slab), bf16),
+            dma((chunks,)),
+            dma((freq_count - 1, chunks)),
+            dma((freq_count - 1, chunks)),
+            dma((levels, chunks)),
+            dma((levels, chunks)),
+            dma((levels, chunks)),
+            dma((levels, chunks)),
+            dma((freq_count - 1, chunks)),
+            dma((freq_count - 1, chunks)),
+            dma((chunks + 1,)),
+        ],
+        compiler_params=pltpu.CompilerParams(
+            collective_id=call_id, has_side_effects=True, vmem_limit_bytes=40 * 2**20
+        ),
+        cost_estimate=pl.CostEstimate(
+            flops=flops, bytes_accessed=2 * green.size, transcendentals=0
+        ),
+    )(spec, green, obs_blocks, inv_blocks)
+
+
+def fits_kernel(chain_shape, green_shape):
+    chains_loc, slab = chain_shape[0], chain_shape[1]
+    param_count = lax.axis_size("param")
+    blocks = CHUNK_FREQS * (green_shape[3] // LANES)
+    return (
+        2 * chains_loc % 16 == 0
+        and slab % LANES == 0
+        and green_shape[3] % LANES == 0
+        and green_shape[1] % CHUNK_FREQS == 0
+        and param_count & (param_count - 1) == 0
+        and param_count > 1
+        and lax.axis_size("freq") > 1
+        and blocks % param_count == 0
+    )
+
+
+def kernel_steps(chain_state, second_moment, noise, green, observed, inv_noise, temper):
+    chains_loc, slab_rows, time_len = chain_state.shape
+    freq_loc, sensors = green.shape[1], green.shape[3]
+    freq_count = lax.axis_size("freq")
+    freq_total = freq_loc * freq_count
+    table = spectral_table(time_len, freq_total)
+    col_blocks = sensors // LANES
+    obs_blocks = (
+        observed.reshape(freq_loc, 2, col_blocks, LANES)
+        .transpose(0, 2, 1, 3)
+        .reshape(freq_loc * col_blocks, 2, LANES)
+    )
+    inv_blocks = inv_noise.reshape(freq_loc * col_blocks, 1, LANES)
+    temper_cols = temper[:, None, None]
+    current = chain_state
+    moment = second_moment
+    for step_num in range(noise.shape[0]):
+        spec = jnp.einsum(
+            "cpt,tj->jcp",
+            current.astype(jnp.bfloat16),
+            table,
+            preferred_element_type=jnp.float32,
+        ).astype(jnp.bfloat16)
+        spec = spec.reshape(freq_count, freq_loc, 2 * chains_loc, slab_rows)
+        own_adjoint = exchange(spec, green, obs_blocks, inv_blocks, step_num)
+        gradient = jnp.einsum(
+            "jcp,tj->cpt",
+            own_adjoint.reshape(2 * freq_total, chains_loc, slab_rows),
+            table,
+            preferred_element_type=jnp.float32,
+        )
+        drift_term = temper_cols * gradient + current
+        moment = decay_rate * moment + (1.0 - decay_rate) * drift_term * drift_term
+        precondition = lax.rsqrt(moment)
+        current = (
+            current
+            - step_length * precondition * drift_term
+            + math.sqrt(2.0 * step_length) * jnp.sqrt(precondition) * noise[step_num]
+        )
+    return (current, moment)
+
+
 def on_device(chain_state, second_moment, noise, green, observed, inv_noise, temper):
+    if fits_kernel(chain_state.shape, green.shape):
+        return kernel_steps(
+            chain_state, second_moment, noise, green, observed, inv_noise, temper
+        )
     chains_loc, slab_rows, time_len = chain_state.shape
     freq_loc = green.shape[1]
     freq_count = lax.axis_size("freq")

time: 238 us -> 116 us (0.49)
  waiting for transfers between devices: 119 us -> 0 us
  Pallas kernels: 0 us -> 90.2 us
  matrix products: 53.1 us -> 17.8 us
  blocking collectives: 31.1 us -> 0 us
  between operations: 14.2 us -> 0.8 us
  other arithmetic: 7.49 us -> 0.62 us
  starting transfers between devices: 5.23 us -> 0 us
    psum x2 -> x0, waiting for transfers between devices: 119 us -> none  [on_device(): lax.psum(partial_data.astype(jnp.bfloat16), 'param').astype(jnp.float32)]
    pallas_call x0 -> x2, Pallas kernels: none -> 90.2 us  [exchange(): pl.pallas_call(functools.partial(exchange_kernel, freq_count, levels, CHU...]
    dot_general x8 -> x4, matrix products: 53.1 us -> 17.8 us  [the longest x2 14 us: kernel_steps(): jnp.einsum('jcp,tj->cpt', own_adjoint.reshape(2 * freq_total, chains_loc,...]
    all_to_all x3 -> x0, blocking collectives: 31.1 us -> none  [the longest x2 21.6 us: on_device(): lax.all_to_all(adjoint, 'freq', split_axis=0, concat_axis=2, tiled=True)]
    squeeze x1 -> x0, local copies, waits for them, and re-layouts: 5.93 us -> none  [on_device(): green_im = green[1]]
    all_to_all x1 -> x0, starting transfers between devices: 5.19 us -> none  [on_device(): lax.all_to_all(local_spec, 'freq', split_axis=2, concat_axis=0, tiled=True)]
    neg x1 -> x0, other arithmetic: 4.41 us -> none  [on_device(): lower_rows = jnp.concatenate([-green_im, green_re], axis=2)]
    convert_element_type x1 -> x0, other arithmetic: 2.46 us -> none  [on_device(): low_state = current.astype(jnp.bfloat16)]
  transfers between devices with their start and end apart: 3 -> 0, of which waited for: 2 -> 0; matrix products, arithmetic and copies ran while one was open for 4% -> 0% of each run, Pallas kernels for 0% -> 0%
where the time goes in v1:
time: 116 us; the launch traced here: 115 us
  Pallas kernels  90.2 us (78%)
  matrix products  17.8 us (15%)
  local copies, waits for them, and re-layouts  5.95 us (5%)
    pallas_call x2, Pallas kernels, exchange(): pl.pallas_call(functools.partial(exchange_kernel, freq_count, levels, CHU...  90.2 us
    dot_general x2, matrix products, kernel_steps(): jnp.einsum('jcp,tj->cpt', own_adjoint.reshape(2 * freq_total, chains_loc,...  14 us
    dot_general x2, matrix products, kernel_steps(): jnp.einsum('cpt,tj->jcp', current.astype(jnp.bfloat16), table, preferred_...  3.84 us
    unnamed x12, local copies, waits for them, and re-layouts  3.4 us

profile of v1, /device:TPU:0, one launch (start us, length us, event | category | flops | bytes accessed | tf_op | source)
XLA Modules:
  0.0 115.4 jit_solution(9620983499773496147)
XLA Ops:
  0.6 0.8 reshape.149.inv_ref
  1.4 0.9 reshape.147
  2.4 0.6 fusion.27
  3.0 0.1 copy.23
  3.1 0.1 reshape.153
  3.2 0.1 convert_element_type.47
  3.3 3.0 %fusion.8 = bf16[128,8,256]{2,0,1:T(8,128)(2,1)S(1)} fusion(bf16[512,128,1]{0,1,2:T(8,128)(2,1)S(1)} %reshape.153, f32[8,256,512]{2,1,0:T(8,128)} %param.7), kind=kOutput, calls=%fused_computation.14 | convolution fusion | flops 269746176 | bytes 4849664 | tf_op jit(solution)/shard_map/cpt,tj->jcp/dot_general | solution.py:324
  6.3 0.3 copy.24
  6.6 0.0 copy-start
  6.6 3.4 %copy-done = bf16[2,16,256,512]{3,2,1,0:T(8,128)(2,1)S(1)} copy-done((bf16[2,16,256,512]{3,2,1,0:T(8,128)(2,1)S(1)}, bf16[2,16,256,512]{3,2,1,0:T(8,128)(2,1)}, u32[]{:S(2)}) %copy-start) | copy-done | bytes 8388632
  10.0 0.0 copy-start.1
  10.0 0.0 copy-start.2
  10.0 0.0 copy-start.3
  10.0 46.7 %shard_map.86 = bf16[4,16,16,256]{3,2,1,0:T(8,128)(2,1)S(1)} custom-call(bf16[4,16,16,256]{3,2,1,0:T(8,128)(2,1)S(1)} %bitcast.36, bf16[2,16,256,512]{3,2,1,0:T(8,128)(2,1)S(1)} %copy-done, f32[64,2,128]{2,1,0:T(2,128)S(1)} %bitcast.37, f32[64,1,128]{2,1,0:T(1,128)S(1)} %reshape.149.inv_ref), custom_call_target="tpu_custom_call" | custom-call | flops 2147483648 | bytes 8388608 | tf_op jit(solution)/shard_map/pallas_call | solution.py:255
  56.6 0.0 slice-start
  56.6 0.0 copy-done.1
  56.7 0.0 copy-done.2
  56.7 0.0 copy-done.3
  56.7 0.0 slice-start.1
  56.7 6.0 %fusion.3 = (f32[8,256,512]{2,1,0:T(8,128)S(1)}, f32[8,256,512]{2,1,0:T(8,128)}) fusion(f32[2,8,256,512]{3,2,1,0:T(8,128)} %param.9, f32[8,256,512]{2,1,0:T(8,128)S(1)} %copy-done.1, f32[8,256,512]{2,1,0:T(8,128)S(1)} %copy-done.2, f32[8]{0:T(128)S(1)} %copy-done.3, bf16[512,128]{0,1:T(8,128)(2,1)S(1)} %convert_element_type.47, ...), kind=kOutput, calls=%fused_computation.7 | convolution fusion | flops 279969792 | bytes 21626912 | tf_op jit(solution)/shard_map/jcp,tj->cpt/dot_general | solution.py:332
  62.7 0.8 fusion.11
  63.5 0.3 copy.28
  63.8 0.0 slice-done
  63.8 0.0 slice-done.1
  63.8 43.5 %shard_map.87 = bf16[4,16,16,256]{3,2,1,0:T(8,128)(2,1)S(1)} custom-call(bf16[4,16,16,256]{3,2,1,0:T(8,128)(2,1)S(1)} %bitcast.35, bf16[2,16,256,512]{3,2,1,0:T(8,128)(2,1)S(1)} %bitcast.32, f32[64,2,128]{2,1,0:T(2,128)S(1)} %bitcast.38, f32[64,1,128]{2,1,0:T(1,128)S(1)} %reshape.149.inv_ref), custom_call_target="tpu_custom_call" | custom-call | flops 2147483648 | bytes 8388608 | tf_op jit(solution)/shard_map/pallas_call | solution.py:255
  107.4 8.0 %fusion.2 = (f32[8,256,512]{2,1,0:T(8,128)}, f32[8,256,512]{2,1,0:T(8,128)}) fusion(f32[2,8,256,512]{3,2,1,0:T(8,128)} %param.9, f32[8,256,512]{2,1,0:T(8,128)S(1)} %get-tuple-element.6, f32[8]{0:T(128)S(1)} %copy-done.3, f32[8,256,512]{2,1,0:T(8,128)S(1)} %copy-done.1, f32[8,256,512]{2,1,0:T(8,128)} %get-tuple-element.7, f32[8,256,512]{2,1,0:T(8,128)S(1)} %copy-done.2, ...), kind=kOutput, calls=%fused_computation.5 | convolution fusion | flops 286261248 | bytes 30015520 | tf_op jit(solution)/shard_map/jcp,tj->cpt/dot_general | solution.py:332
  (4 shorter events, 0.1 us)
Async XLA Ops:
  6.6 3.4 %copy-start = (bf16[2,16,256,512]{3,2,1,0:T(8,128)(2,1)S(1)}, bf16[2,16,256,512]{3,2,1,0:T(8,128)(2,1)}, u32[]{:S(2)}) copy-start(bf16[2,16,256,512]{3,2,1,0:T(8,128)(2,1)} %green_hbm.3) | copy-start | bytes 25165828
  10.0 46.7 %copy-start.1 = (f32[8,256,512]{2,1,0:T(8,128)S(1)}, f32[8,256,512]{2,1,0:T(8,128)}, u32[]{:S(2)}) copy-start(f32[8,256,512]{2,1,0:T(8,128)} %param.7) | copy-start | bytes 12582916
  10.0 46.7 %copy-start.2 = (f32[8,256,512]{2,1,0:T(8,128)S(1)}, f32[8,256,512]{2,1,0:T(8,128)}, u32[]{:S(2)}) copy-start(f32[8,256,512]{2,1,0:T(8,128)} %param.8) | copy-start | bytes 12582916
  10.0 46.7 %copy-start.3 = (f32[8]{0:T(128)S(1)}, f32[8]{0:T(128)}, u32[]{:S(2)}) copy-start(f32[8]{0:T(128)} %param.13) | copy-start | bytes 100
  56.6 7.2 %slice-start = ((s8[8388608]{0:T(1024)(128)(4,1)}), s8[4194304]{0:T(1024)(128)(4,1)S(1)}, s32[]{:S(2)}) async-start(s8[8388608]{0:T(1024)(128)(4,1)} %bitcast.31), calls=%async_computation | async-start | bytes 8388608
  56.7 7.1 %slice-start.1 = ((s8[8388608]{0:T(1024)(128)(4,1)}), s8[4194304]{0:T(1024)(128)(4,1)S(1)}, s32[]{:S(2)}) async-start(s8[8388608]{0:T(1024)(128)(4,1)} %bitcast.31), calls=%async_computation.1 | async-start | bytes 8388608

commit v2 on v1

--- a/solution.py
+++ b/solution.py
@@ -13,6 +13,7 @@
 MESH = pl.DeviceIdType.MESH
 LANES = 128
 CHUNK_FREQS = 2
+STAGE_TICKS = (0, 1, 3, 5, 7, 9, 10)
 
 
 def spectral_table(time_len, freq_total):
@@ -28,11 +29,10 @@
 
 
 def exchange_kernel(
-    freq_count, levels, chunk_freqs,
+    freq_count, chunk_freqs, stage_ticks,
     spec_ref, green_hbm, obs_ref, inv_ref, own_ref,
     green, field, acc, outgoing, incoming, wtd, adj,
-    green_sem, spec_send, spec_recv, red_send, red_recv, gat_send, gat_recv,
-    adj_send, adj_recv, local_sem,
+    green_sem, spec_send, spec_recv, line_send, line_recv, adj_send, adj_recv, local_sem,
 ):
     freq_me = lax.axis_index("freq")
     param_me = lax.axis_index("param")
@@ -42,12 +42,17 @@
     col_blocks = sensors // LANES
     chunk_blocks = chunk_freqs * col_blocks
     chunks = freq_loc // chunk_freqs
-    bits = [lax.rem(param_me // 2**k, 2) for k in range(levels)]
-    partners = [param_me + (1 - 2 * bits[k]) * 2**k for k in range(levels)]
-    lens = [chunk_blocks // 2**k for k in range(levels + 1)]
-    offs = [0]
-    for k in range(levels):
-        offs.append(offs[k] + bits[k] * lens[k + 1])
+    core = lax.rem(param_me, 2)
+    chip = param_me // 2
+    side = chip // 2
+    outer = (chip + side) % 2 == 0
+    inner = (chip + side) % 2 == 1
+    core_peer = param_me + 1 - 2 * core
+    chip_peer = param_me + 2 * (1 - 2 * lax.rem(chip, 2))
+    mid_peer = param_me + 2 * (1 - 2 * side)
+    core_len, mid_len = chunk_blocks // 2, chunk_blocks // 4
+    core_off = core * core_len
+    mid_off = core_off + side * mid_len
 
     def freq_peer(d):
         return lax.rem(freq_me + d, freq_count)
@@ -58,8 +63,12 @@
     barrier = pltpu.get_barrier_semaphore()
     for d in range(1, freq_count):
         pl.semaphore_signal(barrier, inc=1, device_id={"freq": freq_peer(d)}, device_id_type=MESH)
-    for k in range(levels):
-        pl.semaphore_signal(barrier, inc=1, device_id={"param": partners[k]}, device_id_type=MESH)
+    for peer in (core_peer, chip_peer):
+        pl.semaphore_signal(barrier, inc=1, device_id={"param": peer}, device_id_type=MESH)
+
+    @pl.when(inner)
+    def _():
+        pl.semaphore_signal(barrier, inc=1, device_id={"param": mid_peer}, device_id_type=MESH)
 
     def green_copy(i):
         part = pl.ds(i * chunk_freqs, chunk_freqs)
@@ -79,32 +88,39 @@
             device_id_type=MESH,
         )
 
-    def reduce_copy(i, k):
-        part = pl.ds(i * lens[k + 1], lens[k + 1])
-        if k == 0:
-            away = (1 - bits[0]) * lens[1]
-            src = outgoing[0].at[pl.ds(i * chunk_blocks + away, lens[1])]
-        else:
-            src = outgoing[k].at[part]
+    def param_copy(k, i, src, dst, peer):
         return pltpu.make_async_remote_copy(
             src_ref=src,
-            dst_ref=incoming[k].at[part],
-            send_sem=red_send.at[k, i],
-            recv_sem=red_recv.at[k, i],
-            device_id={"param": partners[k]},
+            dst_ref=dst,
+            send_sem=line_send.at[k, i],
+            recv_sem=line_recv.at[k, i],
+            device_id={"param": peer},
             device_id_type=MESH,
         )
 
-    def gather_copy(i, k):
-        part = pl.ds(i * chunk_blocks + offs[k + 1], lens[k + 1])
-        return pltpu.make_async_remote_copy(
-            src_ref=wtd.at[part],
-            dst_ref=wtd.at[part],
-            send_sem=gat_send.at[k, i],
-            recv_sem=gat_recv.at[k, i],
-            device_id={"param": partners[k]},
-            device_id_type=MESH,
-        )
+    def core_reduce(i):
+        src = outgoing[0].at[pl.ds(i * chunk_blocks + (1 - core) * core_len, core_len)]
+        return param_copy(0, i, src, incoming[0].at[pl.ds(i * core_len, core_len)], core_peer)
+
+    def chip_reduce(i):
+        part = pl.ds(i * core_len, core_len)
+        return param_copy(1, i, outgoing[1].at[part], incoming[1].at[part], chip_peer)
+
+    def mid_reduce(i):
+        part = pl.ds(i * mid_len, mid_len)
+        return param_copy(2, i, outgoing[2].at[part], incoming[2].at[part], mid_peer)
+
+    def mid_gather(i):
+        part = wtd.at[pl.ds(i * chunk_blocks + mid_off, mid_len)]
+        return param_copy(3, i, part, part, mid_peer)
+
+    def chip_gather(i):
+        part = wtd.at[pl.ds(i * chunk_blocks + core_off, core_len)]
+        return param_copy(4, i, part, part, chip_peer)
+
+    def core_gather(i):
+        part = wtd.at[pl.ds(i * chunk_blocks + core_off, core_len)]
+        return param_copy(5, i, part, part, core_peer)
 
     def adj_copy(i, d):
         part = pl.ds(i * chunk_freqs, chunk_freqs)
@@ -129,7 +145,7 @@
     def _(i):
         green_copy(i).start()
 
-    pl.semaphore_wait(barrier, freq_count - 1 + levels)
+    pl.semaphore_wait(barrier, freq_count + 1 + (chip + side) % 2)
 
     @pl.loop(0, chunks)
     def _(i):
@@ -163,41 +179,68 @@
                 block = data[:, b * LANES : (b + 1) * LANES]
                 acc[f * col_blocks + b] = block
                 outgoing[0][f * col_blocks + b] = block.astype(jnp.bfloat16)
-        reduce_copy(i, 0).start()
-
-    def reduce(i, k):
-        reduce_copy(i, k - 1).wait_recv()
-        kept = pl.ds(i * chunk_blocks + offs[k], lens[k])
-        acc[kept] = acc[kept] + incoming[k - 1][pl.ds(i * lens[k], lens[k])].astype(jnp.float32)
-        away = offs[k] + (1 - bits[k]) * lens[k + 1]
-        outgoing[k][pl.ds(i * lens[k + 1], lens[k + 1])] = acc[
-            pl.ds(i * chunk_blocks + away, lens[k + 1])
-        ].astype(jnp.bfloat16)
-        reduce_copy(i, k).start()
+        core_reduce(i).start()
+
+    def pass_inward(i):
+        core_reduce(i).wait_recv()
+        kept = pl.ds(i * chunk_blocks + core_off, core_len)
+        part = pl.ds(i * core_len, core_len)
+        total = acc[kept] + incoming[0][part].astype(jnp.float32)
+
+        @pl.when(inner)
+        def _():
+            acc[kept] = total
+
+        @pl.when(outer)
+        def _():
+            outgoing[1][part] = total.astype(jnp.bfloat16)
+            chip_reduce(i).start()
+
+    def cross(i):
+        @pl.when(inner)
+        def _():
+            chip_reduce(i).wait_recv()
+            kept = pl.ds(i * chunk_blocks + core_off, core_len)
+            part = pl.ds(i * core_len, core_len)
+            acc[kept] = acc[kept] + incoming[1][part].astype(jnp.float32)
+            away = pl.ds(i * chunk_blocks + core_off + (1 - side) * mid_len, mid_len)
+            outgoing[2][pl.ds(i * mid_len, mid_len)] = acc[away].astype(jnp.bfloat16)
+            mid_reduce(i).start()
 
     def weigh(i):
-        reduce_copy(i, levels - 1).wait_recv()
-        for n in range(lens[levels]):
-            b = i * chunk_blocks + offs[levels] + n
-            total = acc[b] + incoming[levels - 1][i * lens[levels] + n].astype(jnp.float32)
-            target = obs_ref[b]
-            weight = inv_ref[b]
-            pieces = []
-            for j in range(freq_count):
-                for ri in range(2):
-                    here = j * rows + ri * half_rows
-                    pieces.append(
-                        weight * (total[here : here + half_rows] - target[ri : ri + 1])
-                    )
-            wtd[b] = jnp.concatenate(pieces, axis=0).astype(jnp.bfloat16)
-        gather_copy(i, levels - 1).start()
-
-    def gather(i, k):
-        gather_copy(i, k).wait_recv()
-        gather_copy(i, k - 1).start()
+        @pl.when(inner)
+        def _():
+            mid_reduce(i).wait_recv()
+            for n in range(mid_len):
+                b = i * chunk_blocks + mid_off + n
+                total = acc[b] + incoming[2][i * mid_len + n].astype(jnp.float32)
+                target = obs_ref[b]
+                weight = inv_ref[b]
+                pieces = []
+                for j in range(freq_count):
+                    for ri in range(2):
+                        here = j * rows + ri * half_rows
+                        pieces.append(
+                            weight * (total[here : here + half_rows] - target[ri : ri + 1])
+                        )
+                wtd[b] = jnp.concatenate(pieces, axis=0).astype(jnp.bfloat16)
+            mid_gather(i).start()
+
+    def pass_outward(i):
+        @pl.when(inner)
+        def _():
+            mid_gather(i).wait_recv()
+            chip_gather(i).start()
+            core_gather(i).start()
+
+    def share(i):
+        @pl.when(outer)
+        def _():
+            chip_gather(i).wait_recv()
+            core_gather(i).start()
 
     def backward(i):
-        gather_copy(i, 0).wait_recv()
+        core_gather(i).wait_recv()
         dims = (((1,), (1,)), ((), ()))
         for g in range(chunk_freqs):
             f = i * chunk_freqs + g
@@ -210,17 +253,11 @@
             adj_copy(i, d).start()
         own_adj_copy(i).start()
 
-    stages = [forward]
-    for k in range(1, levels):
-        stages.append(functools.partial(reduce, k=k))
-    stages.append(weigh)
-    for k in range(levels - 1, 0, -1):
-        stages.append(functools.partial(gather, k=k))
-    stages.append(backward)
-
-    @pl.loop(0, chunks + len(stages) - 1)
+    stages = (forward, pass_inward, cross, weigh, pass_outward, share, backward)
+
+    @pl.loop(0, chunks + stage_ticks[-1])
     def _(tick):
-        for lag, stage in enumerate(stages):
+        for lag, stage in zip(stage_ticks, stages):
             @pl.when((tick >= lag) & (tick < chunks + lag))
             def _():
                 stage(tick - lag)
@@ -229,9 +266,19 @@
     def _(i):
         for d in range(1, freq_count):
             spec_copy(i, d).wait_send()
-        for k in range(levels):
-            reduce_copy(i, k).wait_send()
-            gather_copy(i, k).wait_send()
+        core_reduce(i).wait_send()
+        core_gather(i).wait_send()
+
+        @pl.when(outer)
+        def _():
+            chip_reduce(i).wait_send()
+
+        @pl.when(inner)
+        def _():
+            mid_reduce(i).wait_send()
+            mid_gather(i).wait_send()
+            chip_gather(i).wait_send()
+
         for d in range(1, freq_count):
             adj_copy(i, d).wait_send()
             adj_copy(i, d).wait_recv()
@@ -240,7 +287,6 @@
 
 def exchange(spec, green, obs_blocks, inv_blocks, call_id):
     freq_count, freq_loc, rows, slab = spec.shape
-    levels = int(math.log2(lax.axis_size("param")))
     sensors = green.shape[3]
     col_blocks = sensors // LANES
     chunk_blocks = CHUNK_FREQS * col_blocks
@@ -248,33 +294,27 @@
     blocks = freq_loc * col_blocks
     all_rows = freq_count * rows
     bf16, f32 = jnp.bfloat16, jnp.float32
-    piece = [blocks // 2 ** (k + 1) for k in range(levels)]
     dma = pltpu.SemaphoreType.DMA
     vmem = pl.BlockSpec(memory_space=pltpu.VMEM)
     flops = 16 * freq_loc * all_rows * slab * sensors
     return pl.pallas_call(
-        functools.partial(exchange_kernel, freq_count, levels, CHUNK_FREQS),
+        functools.partial(exchange_kernel, freq_count, CHUNK_FREQS, STAGE_TICKS),
         out_shape=jax.ShapeDtypeStruct(spec.shape, bf16),
-        in_specs=[vmem, pl.BlockSpec(memory_space=pl.ANY), vmem, vmem],
+        in_specs=[vmem, pl.BlockSpec(memory_space=pltpu.HBM), vmem, vmem],
         out_specs=vmem,
         scratch_shapes=[
             pltpu.VMEM(green.shape, bf16),
             pltpu.VMEM((freq_loc, freq_count, rows, slab), bf16),
             pltpu.VMEM((blocks, all_rows, LANES), f32),
-            [
-                pltpu.VMEM((blocks if k == 0 else piece[k], all_rows, LANES), bf16)
-                for k in range(levels)
-            ],
-            [pltpu.VMEM((piece[k], all_rows, LANES), bf16) for k in range(levels)],
+            [pltpu.VMEM((blocks // part, all_rows, LANES), bf16) for part in (1, 2, 4)],
+            [pltpu.VMEM((blocks // part, all_rows, LANES), bf16) for part in (2, 2, 4)],
             pltpu.VMEM((blocks, all_rows, LANES), bf16),
             pltpu.VMEM((freq_loc, freq_count, rows, slab), bf16),
             dma((chunks,)),
             dma((freq_count - 1, chunks)),
             dma((freq_count - 1, chunks)),
-            dma((levels, chunks)),
-            dma((levels, chunks)),
-            dma((levels, chunks)),
-            dma((levels, chunks)),
+            dma((6, chunks)),
+            dma((6, chunks)),
             dma((freq_count - 1, chunks)),
             dma((freq_count - 1, chunks)),
             dma((chunks + 1,)),
@@ -297,10 +337,9 @@
         and slab % LANES == 0
         and green_shape[3] % LANES == 0
         and green_shape[1] % CHUNK_FREQS == 0
-        and param_count & (param_count - 1) == 0
-        and param_count > 1
+        and param_count == 8
         and lax.axis_size("freq") > 1
-        and blocks % param_count == 0
+        and blocks % 4 == 0
     )
 
 

time: 116 us -> 101 us (0.87)
  Pallas kernels: 90.2 us -> 75.3 us
    pallas_call x2, Pallas kernels: 90.2 us -> 75.3 us  [exchange(): pl.pallas_call(functools.partial(exchange_kernel, freq_count, CHUNK_FREQS...]
where the time goes in v2:
time: 101 us; the launch traced here: 100 us
  Pallas kernels  75.3 us (75%)
  matrix products  17.8 us (18%)
  local copies, waits for them, and re-layouts  5.95 us (6%)
    pallas_call x2, Pallas kernels, exchange(): pl.pallas_call(functools.partial(exchange_kernel, freq_count, CHUNK_FREQS...  75.3 us
    dot_general x2, matrix products, kernel_steps(): jnp.einsum('jcp,tj->cpt', own_adjoint.reshape(2 * freq_total, chains_loc,...  14 us
    dot_general x2, matrix products, kernel_steps(): jnp.einsum('cpt,tj->jcp', current.astype(jnp.bfloat16), table, preferred_...  3.84 us
    unnamed x12, local copies, waits for them, and re-layouts  3.4 us

profile of v2, /device:TPU:0, one launch (start us, length us, event | category | flops | bytes accessed | tf_op | source)
XLA Modules:
  0.0 100.5 jit_solution(5685828114704077304)
XLA Ops:
  0.6 0.8 reshape.149.inv_ref
  1.4 0.9 reshape.147
  2.4 0.6 fusion.27
  3.0 0.1 copy.23
  3.1 0.1 reshape.153
  3.2 0.1 convert_element_type.47
  3.3 3.0 %fusion.8 = bf16[128,8,256]{2,0,1:T(8,128)(2,1)S(1)} fusion(bf16[512,128,1]{0,1,2:T(8,128)(2,1)S(1)} %reshape.153, f32[8,256,512]{2,1,0:T(8,128)} %param.7), kind=kOutput, calls=%fused_computation.14 | convolution fusion | flops 269746176 | bytes 4849664 | tf_op jit(solution)/shard_map/cpt,tj->jcp/dot_general | solution.py:363
  6.3 0.3 copy.24
  6.6 0.0 copy-start
  6.6 3.4 %copy-done = bf16[2,16,256,512]{3,2,1,0:T(8,128)(2,1)S(1)} copy-done((bf16[2,16,256,512]{3,2,1,0:T(8,128)(2,1)S(1)}, bf16[2,16,256,512]{3,2,1,0:T(8,128)(2,1)}, u32[]{:S(2)}) %copy-start) | copy-done | bytes 8388632
  10.0 0.0 copy-start.1
  10.0 0.0 copy-start.2
  10.0 0.0 copy-start.3
  10.0 40.0 %shard_map.86 = bf16[4,16,16,256]{3,2,1,0:T(8,128)(2,1)S(1)} custom-call(bf16[4,16,16,256]{3,2,1,0:T(8,128)(2,1)S(1)} %bitcast.36, bf16[2,16,256,512]{3,2,1,0:T(8,128)(2,1)S(1)} %copy-done, f32[64,2,128]{2,1,0:T(2,128)S(1)} %bitcast.37, f32[64,1,128]{2,1,0:T(1,128)S(1)} %reshape.149.inv_ref), custom_call_target="tpu_custom_call" | custom-call | flops 2147483648 | bytes 8388608 | tf_op jit(solution)/shard_map/pallas_call | solution.py:300
  50.0 0.0 slice-start
  50.0 0.0 copy-done.1
  50.0 0.0 copy-done.2
  50.0 0.0 copy-done.3
  50.1 0.0 slice-start.1
  50.1 6.0 %fusion.3 = (f32[8,256,512]{2,1,0:T(8,128)S(1)}, f32[8,256,512]{2,1,0:T(8,128)}) fusion(f32[2,8,256,512]{3,2,1,0:T(8,128)} %param.9, f32[8,256,512]{2,1,0:T(8,128)S(1)} %copy-done.1, f32[8,256,512]{2,1,0:T(8,128)S(1)} %copy-done.2, f32[8]{0:T(128)S(1)} %copy-done.3, bf16[512,128]{0,1:T(8,128)(2,1)S(1)} %convert_element_type.47, ...), kind=kOutput, calls=%fused_computation.7 | convolution fusion | flops 279969792 | bytes 21626912 | tf_op jit(solution)/shard_map/jcp,tj->cpt/dot_general | solution.py:371
  56.1 0.8 fusion.11
  56.9 0.3 copy.28
  57.2 0.0 slice-done
  57.2 0.0 slice-done.1
  57.2 35.3 %shard_map.87 = bf16[4,16,16,256]{3,2,1,0:T(8,128)(2,1)S(1)} custom-call(bf16[4,16,16,256]{3,2,1,0:T(8,128)(2,1)S(1)} %bitcast.35, bf16[2,16,256,512]{3,2,1,0:T(8,128)(2,1)S(1)} %bitcast.32, f32[64,2,128]{2,1,0:T(2,128)S(1)} %bitcast.38, f32[64,1,128]{2,1,0:T(1,128)S(1)} %reshape.149.inv_ref), custom_call_target="tpu_custom_call" | custom-call | flops 2147483648 | bytes 8388608 | tf_op jit(solution)/shard_map/pallas_call | solution.py:300
  92.5 8.0 %fusion.2 = (f32[8,256,512]{2,1,0:T(8,128)}, f32[8,256,512]{2,1,0:T(8,128)}) fusion(f32[2,8,256,512]{3,2,1,0:T(8,128)} %param.9, f32[8,256,512]{2,1,0:T(8,128)S(1)} %get-tuple-element.6, f32[8]{0:T(128)S(1)} %copy-done.3, f32[8,256,512]{2,1,0:T(8,128)S(1)} %copy-done.1, f32[8,256,512]{2,1,0:T(8,128)} %get-tuple-element.7, f32[8,256,512]{2,1,0:T(8,128)S(1)} %copy-done.2, ...), kind=kOutput, calls=%fused_computation.5 | convolution fusion | flops 286261248 | bytes 30015520 | tf_op jit(solution)/shard_map/jcp,tj->cpt/dot_general | solution.py:371
  (4 shorter events, 0.1 us)
Async XLA Ops:
  6.6 3.4 %copy-start = (bf16[2,16,256,512]{3,2,1,0:T(8,128)(2,1)S(1)}, bf16[2,16,256,512]{3,2,1,0:T(8,128)(2,1)}, u32[]{:S(2)}) copy-start(bf16[2,16,256,512]{3,2,1,0:T(8,128)(2,1)} %green_hbm.3) | copy-start | bytes 25165828
  10.0 40.1 %copy-start.1 = (f32[8,256,512]{2,1,0:T(8,128)S(1)}, f32[8,256,512]{2,1,0:T(8,128)}, u32[]{:S(2)}) copy-start(f32[8,256,512]{2,1,0:T(8,128)} %param.7) | copy-start | bytes 12582916
  10.0 40.1 %copy-start.2 = (f32[8,256,512]{2,1,0:T(8,128)S(1)}, f32[8,256,512]{2,1,0:T(8,128)}, u32[]{:S(2)}) copy-start(f32[8,256,512]{2,1,0:T(8,128)} %param.8) | copy-start | bytes 12582916
  10.0 40.1 %copy-start.3 = (f32[8]{0:T(128)S(1)}, f32[8]{0:T(128)}, u32[]{:S(2)}) copy-start(f32[8]{0:T(128)} %param.13) | copy-start | bytes 100
  50.0 7.2 %slice-start = ((s8[8388608]{0:T(1024)(128)(4,1)}), s8[4194304]{0:T(1024)(128)(4,1)S(1)}, s32[]{:S(2)}) async-start(s8[8388608]{0:T(1024)(128)(4,1)} %bitcast.31), calls=%async_computation | async-start | bytes 8388608
  50.1 7.1 %slice-start.1 = ((s8[8388608]{0:T(1024)(128)(4,1)}), s8[4194304]{0:T(1024)(128)(4,1)S(1)}, s32[]{:S(2)}) async-start(s8[8388608]{0:T(1024)(128)(4,1)} %bitcast.31), calls=%async_computation.1 | async-start | bytes 8388608

commit v3 on v2

--- a/solution.py
+++ b/solution.py
@@ -31,7 +31,7 @@
 def exchange_kernel(
     freq_count, chunk_freqs, stage_ticks,
     spec_ref, green_hbm, obs_ref, inv_ref, own_ref,
-    green, field, acc, outgoing, incoming, wtd, adj,
+    obs_blocks, inv_blocks, green, field, acc, outgoing, incoming, wtd, adj,
     green_sem, spec_send, spec_recv, line_send, line_recv, adj_send, adj_recv, local_sem,
 ):
     freq_me = lax.axis_index("freq")
@@ -145,6 +145,14 @@
     def _(i):
         green_copy(i).start()
 
+    for f in range(freq_loc):
+        for b in range(col_blocks):
+            lanes = slice(b * LANES, (b + 1) * LANES)
+            inv_blocks[f * col_blocks + b] = inv_ref[f : f + 1, lanes]
+            for ri in range(2):
+                lanes = slice(ri * sensors + b * LANES, ri * sensors + (b + 1) * LANES)
+                obs_blocks[f * col_blocks + b, ri : ri + 1] = obs_ref[f : f + 1, lanes]
+
     pl.semaphore_wait(barrier, freq_count + 1 + (chip + side) % 2)
 
     @pl.loop(0, chunks)
@@ -214,8 +222,8 @@
             for n in range(mid_len):
                 b = i * chunk_blocks + mid_off + n
                 total = acc[b] + incoming[2][i * mid_len + n].astype(jnp.float32)
-                target = obs_ref[b]
-                weight = inv_ref[b]
+                target = obs_blocks[b]
+                weight = inv_blocks[b]
                 pieces = []
                 for j in range(freq_count):
                     for ri in range(2):
@@ -285,7 +293,7 @@
         own_adj_copy(i).wait()
 
 
-def exchange(spec, green, obs_blocks, inv_blocks, call_id):
+def exchange(spec, green, observed, inv_noise, call_id):
     freq_count, freq_loc, rows, slab = spec.shape
     sensors = green.shape[3]
     col_blocks = sensors // LANES
@@ -303,6 +311,8 @@
         in_specs=[vmem, pl.BlockSpec(memory_space=pltpu.HBM), vmem, vmem],
         out_specs=vmem,
         scratch_shapes=[
+            pltpu.VMEM((blocks, 2, LANES), f32),
+            pltpu.VMEM((blocks, 1, LANES), f32),
             pltpu.VMEM(green.shape, bf16),
             pltpu.VMEM((freq_loc, freq_count, rows, slab), bf16),
             pltpu.VMEM((blocks, all_rows, LANES), f32),
@@ -320,12 +330,12 @@
             dma((chunks + 1,)),
         ],
         compiler_params=pltpu.CompilerParams(
-            collective_id=call_id, has_side_effects=True, vmem_limit_bytes=40 * 2**20
+            collective_id=call_id, has_side_effects=True, vmem_limit_bytes=20 * 2**20
         ),
         cost_estimate=pl.CostEstimate(
             flops=flops, bytes_accessed=2 * green.size, transcendentals=0
         ),
-    )(spec, green, obs_blocks, inv_blocks)
+    )(spec, green, observed, inv_noise)
 
 
 def fits_kernel(chain_shape, green_shape):
@@ -345,17 +355,10 @@
 
 def kernel_steps(chain_state, second_moment, noise, green, observed, inv_noise, temper):
     chains_loc, slab_rows, time_len = chain_state.shape
-    freq_loc, sensors = green.shape[1], green.shape[3]
+    freq_loc = green.shape[1]
     freq_count = lax.axis_size("freq")
     freq_total = freq_loc * freq_count
     table = spectral_table(time_len, freq_total)
-    col_blocks = sensors // LANES
-    obs_blocks = (
-        observed.reshape(freq_loc, 2, col_blocks, LANES)
-        .transpose(0, 2, 1, 3)
-        .reshape(freq_loc * col_blocks, 2, LANES)
-    )
-    inv_blocks = inv_noise.reshape(freq_loc * col_blocks, 1, LANES)
     temper_cols = temper[:, None, None]
     current = chain_state
     moment = second_moment
@@ -367,7 +370,7 @@
             preferred_element_type=jnp.float32,
         ).astype(jnp.bfloat16)
         spec = spec.reshape(freq_count, freq_loc, 2 * chains_loc, slab_rows)
-        own_adjoint = exchange(spec, green, obs_blocks, inv_blocks, step_num)
+        own_adjoint = exchange(spec, green, observed, inv_noise, step_num)
         gradient = jnp.einsum(
             "jcp,tj->cpt",
             own_adjoint.reshape(2 * freq_total, chains_loc, slab_rows),

time: 101 us -> 97.1 us (0.961)
  matrix products: 17.8 us -> 16 us
  local copies, waits for them, and re-layouts: 5.95 us -> 4.25 us
    dot_general x2, matrix products: 14 us -> 12.1 us  [kernel_steps(): jnp.einsum('jcp,tj->cpt', own_adjoint.reshape(2 * freq_total, chains_loc,...]
    reshape x3 -> x0, local copies, waits for them, and re-layouts: 1.71 us -> none  [the longest x2 0.91 us: kernel_steps(): observed.reshape(freq_loc, 2, col_blocks, LANES).transpose(0, 2, 1, 3)]
    unnamed x12 -> x16, local copies, waits for them, and re-layouts: 3.4 us -> 3.41 us
where the time goes in v3:
time: 97.1 us; the launch traced here: 96.9 us
  Pallas kernels  75.3 us (78%)
  matrix products  16 us (16%)
  local copies, waits for them, and re-layouts  4.25 us (4%)
    pallas_call x2, Pallas kernels, exchange(): pl.pallas_call(functools.partial(exchange_kernel, freq_count, CHUNK_FREQS...  75.3 us
    dot_general x2, matrix products, kernel_steps(): jnp.einsum('jcp,tj->cpt', own_adjoint.reshape(2 * freq_total, chains_loc,...  12.1 us
    dot_general x2, matrix products, kernel_steps(): jnp.einsum('cpt,tj->jcp', current.astype(jnp.bfloat16), table, preferred_...  3.84 us
    unnamed x16, local copies, waits for them, and re-layouts  3.41 us

profile of v3, /device:TPU:0, one launch (start us, length us, event | category | flops | bytes accessed | tf_op | source)
XLA Modules:
  0.0 96.9 jit_solution(9474295912818922042)
XLA Ops:
  0.6 0.0 copy-start.2
  0.6 0.0 copy-start.1
  0.7 0.6 fusion.27
  1.3 0.1 copy.21
  1.4 0.1 reshape.141
  1.5 0.1 convert_element_type.47
  1.6 3.0 %fusion.8 = bf16[128,8,256]{2,0,1:T(8,128)(2,1)S(1)} fusion(bf16[512,128,1]{0,1,2:T(8,128)(2,1)S(1)} %reshape.141, f32[8,256,512]{2,1,0:T(8,128)} %param.7), kind=kOutput, calls=%fused_computation.14 | convolution fusion | flops 269746176 | bytes 4849664 | tf_op jit(solution)/shard_map/cpt,tj->jcp/dot_general | solution.py:366
  4.6 0.3 copy.22
  4.9 0.0 copy-done.2
  4.9 0.0 copy-done.1
  4.9 0.0 copy-start
  4.9 3.4 %copy-done = bf16[2,16,256,512]{3,2,1,0:T(8,128)(2,1)S(1)} copy-done((bf16[2,16,256,512]{3,2,1,0:T(8,128)(2,1)S(1)}, bf16[2,16,256,512]{3,2,1,0:T(8,128)(2,1)}, u32[]{:S(2)}) %copy-start) | copy-done | bytes 8388632
  8.3 0.0 copy-start.3
  8.3 0.0 copy-start.4
  8.3 0.0 copy-start.5
  8.3 40.0 %shard_map.86 = bf16[4,16,16,256]{3,2,1,0:T(8,128)(2,1)S(1)} custom-call(bf16[4,16,16,256]{3,2,1,0:T(8,128)(2,1)S(1)} %bitcast.32, bf16[2,16,256,512]{3,2,1,0:T(8,128)(2,1)S(1)} %copy-done, f32[16,1024]{1,0:T(8,128)S(1)} %copy-done.1, f32[16,512]{1,0:T(8,128)S(1)} %copy-done.2), custom_call_target="tpu_custom_call" | custom-call | flops 2147483648 | bytes 8388608 | tf_op jit(solution)/shard_map/pallas_call | solution.py:308
  48.3 0.0 slice-start
  48.3 0.0 copy-done.3
  48.3 0.0 copy-done.4
  48.3 0.0 copy-done.5
  48.4 0.0 slice-start.1
  48.4 4.8 %fusion.3 = (f32[8,256,512]{2,1,0:T(8,128)S(1)}, f32[8,256,512]{2,1,0:T(8,128)S(1)}) fusion(f32[2,8,256,512]{3,2,1,0:T(8,128)} %param.9, f32[8,256,512]{2,1,0:T(8,128)S(1)} %copy-done.3, f32[8,256,512]{2,1,0:T(8,128)S(1)} %copy-done.4, f32[8]{0:T(128)S(1)} %copy-done.5, bf16[512,128]{0,1:T(8,128)(2,1)S(1)} %convert_element_type.47, ...), kind=kOutput, calls=%fused_computation.7 | convolution fusion | flops 279969792 | bytes 21626912 | tf_op jit(solution)/shard_map/jcp,tj->cpt/dot_general | solution.py:374
  53.2 0.8 fusion.11
  54.0 0.3 copy.25
  54.3 0.0 slice-done
  54.3 0.0 slice-done.1
  54.3 35.3 %shard_map.87 = bf16[4,16,16,256]{3,2,1,0:T(8,128)(2,1)S(1)} custom-call(bf16[4,16,16,256]{3,2,1,0:T(8,128)(2,1)S(1)} %bitcast.33, bf16[2,16,256,512]{3,2,1,0:T(8,128)(2,1)S(1)} %bitcast.29, f32[16,1024]{1,0:T(8,128)S(1)} %copy-done.1, f32[16,512]{1,0:T(8,128)S(1)} %copy-done.2), custom_call_target="tpu_custom_call" | custom-call | flops 2147483648 | bytes 8388608 | tf_op jit(solution)/shard_map/pallas_call | solution.py:308
  89.6 7.3 %fusion.2 = (f32[8,256,512]{2,1,0:T(8,128)}, f32[8,256,512]{2,1,0:T(8,128)}) fusion(f32[2,8,256,512]{3,2,1,0:T(8,128)} %param.9, f32[8,256,512]{2,1,0:T(8,128)S(1)} %get-tuple-element.6, f32[8]{0:T(128)S(1)} %copy-done.5, f32[8,256,512]{2,1,0:T(8,128)S(1)} %copy-done.3, f32[8,256,512]{2,1,0:T(8,128)S(1)} %get-tuple-element.7, ...), kind=kOutput, calls=%fused_computation.5 | convolution fusion | flops 286261248 | bytes 30015520 | tf_op jit(solution)/shard_map/jcp,tj->cpt/dot_general | solution.py:374
  (3 shorter events, 0.0 us)
Async XLA Ops:
  0.6 4.3 %copy-start.2 = (f32[16,512]{1,0:T(8,128)S(1)}, f32[16,512]{1,0:T(8,128)}, u32[]{:S(2)}) copy-start(f32[16,512]{1,0:T(8,128)} %inv_ref.3) | copy-start | bytes 98308
  0.6 4.3 %copy-start.1 = (f32[16,1024]{1,0:T(8,128)S(1)}, f32[16,1024]{1,0:T(8,128)}, u32[]{:S(2)}) copy-start(f32[16,1024]{1,0:T(8,128)} %obs_ref.3) | copy-start | bytes 196612
  4.9 3.4 %copy-start = (bf16[2,16,256,512]{3,2,1,0:T(8,128)(2,1)S(1)}, bf16[2,16,256,512]{3,2,1,0:T(8,128)(2,1)}, u32[]{:S(2)}) copy-start(bf16[2,16,256,512]{3,2,1,0:T(8,128)(2,1)} %green_hbm.3) | copy-start | bytes 25165828
  8.3 40.0 %copy-start.3 = (f32[8,256,512]{2,1,0:T(8,128)S(1)}, f32[8,256,512]{2,1,0:T(8,128)}, u32[]{:S(2)}) copy-start(f32[8,256,512]{2,1,0:T(8,128)} %param.7) | copy-start | bytes 12582916
  8.3 40.0 %copy-start.4 = (f32[8,256,512]{2,1,0:T(8,128)S(1)}, f32[8,256,512]{2,1,0:T(8,128)}, u32[]{:S(2)}) copy-start(f32[8,256,512]{2,1,0:T(8,128)} %param.8) | copy-start | bytes 12582916
  8.3 40.1 %copy-start.5 = (f32[8]{0:T(128)S(1)}, f32[8]{0:T(128)}, u32[]{:S(2)}) copy-start(f32[8]{0:T(128)} %param.13) | copy-start | bytes 100
  48.3 6.0 %slice-start = ((s8[8388608]{0:T(1024)(128)(4,1)}), s8[4194304]{0:T(1024)(128)(4,1)S(1)}, s32[]{:S(2)}) async-start(s8[8388608]{0:T(1024)(128)(4,1)} %bitcast.28), calls=%async_computation | async-start | bytes 8388608
  48.4 5.9 %slice-start.1 = ((s8[8388608]{0:T(1024)(128)(4,1)}), s8[4194304]{0:T(1024)(128)(4,1)S(1)}, s32[]{:S(2)}) async-start(s8[8388608]{0:T(1024)(128)(4,1)} %bitcast.28), calls=%async_computation.1 | async-start | bytes 8388608
